TPU v7x, 256 devices: a whole 4x4x8 slice. The times are simulated.
256 devices in a mesh: grp: 4 (over y), seq: 16 (over z, core), head: 4 (over x).
Axes of the slice: x: 4, y: 4, z: 8, core: 2. Of those that a mesh axis runs over, the one named last changes fastest.
Arguments:
- keys: bfloat16 [32, 8192, 1536], P('grp', 'seq', 'head'), may hold values from -6 to 6
- values: bfloat16 [32, 8192, 1536], P('grp', 'seq', 'head'), may hold values from -6 to 6
- log_forget: float32 [32, 24, 8192], P('grp', 'head', 'seq'), may hold values from -0.6 to 0, as said below
- keep: int32 [32, 8192], P('grp', 'seq'), may hold values from 0 to 1, as said below
- merge_weight: float32 [32, 8192], P('grp', 'seq'), may hold values from 0.1 to 10
- lengths: int32 [32], P('grp'), may hold values from 64 to 8192, as said below
- route: int32 [32], P('grp'), may hold values from 0 to 31, as said below
- fresh: bfloat16 [3, 32, 1536], P(None, 'grp', 'head'), may hold values from -7.5 to 7.5
- new_forget: bfloat16 [32, 24], P('grp', 'head'), may hold values from -1 to -0.049804688
- out_weight: bfloat16 [1536, 1536], P('head', 'seq'), may hold values from -0.15625 to 0.15625
Outputs:
- compact_keys: bfloat16 [32, 4096, 1536], P('grp', 'seq', 'head')
- compact_values: bfloat16 [32, 4096, 1536], P('grp', 'seq', 'head')
- compact_decay: float32 [32, 24, 4096], P('grp', 'head', 'seq')
- layer_out: bfloat16 [32, 1536], P('grp', 'seq')
Inputs may be any that keep to these rules, and one draw needn't show every extreme that they name: `keep`: within every aligned block of 64 positions of a request, between 16 and 31 entries are 1, and some block has exactly 31. `lengths`: multiples of 64; the first request of every 8 in order has 8192. `route`: A permutation of the requests. `log_forget`: Negative.
All inputs are finite; a program needn't handle non-finite values.
Results may differ from a plain program's by a relative error of at most 0.0085.
Values may be sent and summed in bfloat16 or wider, within the bound.
A program may use at most 64 MiB of HBM per device.

v0:
```python
import jax
import jax.numpy as jnp
from jax import lax
from jax.sharding import PartitionSpec as P

BLOCK = 64
SLOTS = 32
EMPTY_LOG = -10000.0


def carried_in(value, axis, join, neutral):
    count, mine = (lax.axis_size(axis), lax.axis_index(axis))
    pieces = lax.all_gather(value, axis)
    pieces = pieces[::-1]
    mine = count - 1 - mine
    so_far = jnp.full_like(value, 0) + jnp.asarray(neutral, value.dtype)

    def turn(position, so_far):
        longer = join(so_far, pieces[position])
        return jnp.where(position < mine, longer, so_far)

    return lax.fori_loop(0, count - 1, turn, so_far)


def merged(value, axis, join):
    pieces = jax.tree.map(lambda part: lax.all_gather(part, axis), value)
    head = jax.tree.map(lambda part: part[0], pieces)
    tail = jax.tree.map(lambda part: part[1:], pieces)
    so_far, _ = lax.scan(lambda so_far, section: (join(so_far, section), None), head, tail)
    return so_far


def add_totals(earlier, later):
    return earlier + later


def merge_parts(first, second):
    top_one, sum_one, acc_one = first
    top_two, sum_two, acc_two = second
    joint = jnp.maximum(top_one, top_two)
    scale_one = jnp.exp(top_one - joint)
    scale_two = jnp.exp(top_two - joint)
    return (
        joint,
        sum_one * scale_one + sum_two * scale_two,
        acc_one * scale_one[..., None] + acc_two * scale_two[..., None],
    )


def shards(
    keys, values, log_forget, keep, merge_weight, lengths, route, fresh, new_forget, out_weight
):
    req_dev, pos_dev, width_dev = keys.shape
    heads_dev = log_forget.shape[1]
    head_size = width_dev // heads_dev
    blocks_dev = pos_dev // BLOCK
    rows_dev = blocks_dev * SLOTS
    shard = lax.axis_index("seq")
    position = shard * pos_dev + jnp.arange(pos_dev, dtype=jnp.int32)
    live = position[None, :] < lengths[:, None]
    forget = jnp.where(live[:, None, :], log_forget, 0.0)
    own_total = jnp.sum(forget, axis=2)
    inner = own_total[:, :, None] - jnp.cumsum(forget, axis=2)
    later_sum = carried_in(own_total, "seq", add_totals, jnp.zeros_like(own_total))
    log_decay = inner + later_sum[:, :, None]
    flags = keep.reshape(req_dev, blocks_dev, BLOCK)
    rank = jnp.cumsum(flags, axis=2) - 1
    slot_ids = jnp.arange(SLOTS - 1, dtype=jnp.int32)
    block_start = shard * pos_dev + jnp.arange(blocks_dev, dtype=jnp.int32) * BLOCK
    block_live = (block_start[None, :] < lengths[:, None]).astype(jnp.float32)
    chosen = (
        (flags[:, :, None, :] == 1) & (rank[:, :, None, :] == slot_ids[None, None, :, None])
    ).astype(jnp.float32)
    chosen = chosen * block_live[:, :, None, None]
    dropped = flags == 0
    weighted = jnp.where(dropped, merge_weight.reshape(req_dev, blocks_dev, BLOCK), 0.0)
    share = (
        (weighted / jnp.sum(weighted, axis=2, keepdims=True))
        .astype(jnp.bfloat16)
        .astype(jnp.float32)
    )
    merged_row = (share * block_live[:, :, None])[:, :, None, :]
    select = jnp.concatenate([chosen, merged_row], axis=2).astype(jnp.bfloat16)
    key_blocks = keys.reshape(req_dev, blocks_dev, BLOCK, width_dev)
    value_blocks = values.reshape(req_dev, blocks_dev, BLOCK, width_dev)
    packed_keys = (
        jnp.einsum("rbej,rbjc->rbec", select, key_blocks, preferred_element_type=jnp.float32)
        .astype(jnp.bfloat16)
        .reshape(req_dev, rows_dev, width_dev)
    )
    packed_values = (
        jnp.einsum("rbej,rbjc->rbec", select, value_blocks, preferred_element_type=jnp.float32)
        .astype(jnp.bfloat16)
        .reshape(req_dev, rows_dev, width_dev)
    )
    decay_blocks = log_decay.reshape(req_dev, heads_dev, blocks_dev, BLOCK)
    kept_log = jnp.einsum("rbej,rhbj->rhbe", chosen, decay_blocks, precision=lax.Precision.HIGHEST)
    filled = jnp.sum(chosen, axis=3)
    kept_log = kept_log + (1.0 - filled)[:, None, :, :] * EMPTY_LOG
    drop_mask = dropped[:, None, :, :]
    drop_peak = jnp.max(jnp.where(drop_mask, decay_blocks, -jnp.inf), axis=3)
    spread = jnp.where(drop_mask, jnp.exp(decay_blocks - drop_peak[..., None]), 0.0)
    merged_log = drop_peak + jnp.log(jnp.sum(share[:, None, :, :] * spread, axis=3))
    merged_log = jnp.where(block_live[:, None, :] > 0, merged_log, EMPTY_LOG)
    slot_log = jnp.concatenate([kept_log, merged_log[..., None]], axis=3).reshape(
        req_dev, heads_dev, rows_dev
    )
    compact_decay = jnp.exp(slot_log)
    dealt_keys, dealt_values = (
        lax.all_to_all(packed_keys, "seq", split_axis=1, concat_axis=1, tiled=True),
        lax.all_to_all(packed_values, "seq", split_axis=1, concat_axis=1, tiled=True),
    )
    arrived, arrived_forget = (
        lax.all_gather(fresh, "grp", axis=1, tiled=True),
        lax.all_gather(new_forget, "grp", axis=0, tiled=True),
    )
    picked = jnp.take(arrived, route, axis=1)
    new_log = jnp.take(arrived_forget, route, axis=0).astype(jnp.float32)
    query = picked[0].reshape(req_dev, heads_dev, head_size)
    own_key = picked[1].reshape(req_dev, heads_dev, head_size)
    own_value = picked[2].reshape(req_dev, heads_dev, head_size).astype(jnp.float32)
    scale = head_size ** (-0.5)
    key_rows = packed_keys.reshape(req_dev, rows_dev, heads_dev, head_size)
    value_rows = packed_values.reshape(req_dev, rows_dev, heads_dev, head_size)
    scores = (
        jnp.einsum("rhd,rnhd->rhn", query, key_rows, preferred_element_type=jnp.float32) * scale
        + slot_log
    )
    local_top = jnp.max(scores, axis=2)
    weights = jnp.exp(scores - local_top[..., None]).astype(jnp.bfloat16)
    local_sum = jnp.sum(weights.astype(jnp.float32), axis=2)
    local_acc = jnp.einsum("rhn,rnhd->rhd", weights, value_rows, preferred_element_type=jnp.float32)
    top, total_sum, total_acc = merged((local_top, local_sum, local_acc), "seq", merge_parts)
    own_score = jnp.sum(query.astype(jnp.float32) * own_key.astype(jnp.float32), axis=2) * scale
    cache_top = top + new_log
    joint = jnp.maximum(cache_top, own_score)
    cache_scale = jnp.exp(cache_top - joint)
    self_weight = jnp.exp(own_score - joint)
    attended = (cache_scale[..., None] * total_acc + self_weight[..., None] * own_value) / (
        cache_scale * total_sum + self_weight
    )[..., None]
    attended = attended.reshape(req_dev, width_dev).astype(jnp.bfloat16)
    partial_out = jnp.dot(attended, out_weight, preferred_element_type=jnp.float32)
    layer_out = lax.psum(partial_out, "head").astype(jnp.bfloat16)
    return (dealt_keys, dealt_values, compact_decay, layer_out)


def solution(mesh):
    return jax.shard_map(
        shards,
        mesh=mesh,
        in_specs=(
            P("grp", "seq", "head"),
            P("grp", "seq", "head"),
            P("grp", "head", "seq"),
            P("grp", "seq"),
            P("grp", "seq"),
            P("grp"),
            P("grp"),
            P(None, "grp", "head"),
            P("grp", "head"),
            P("head", "seq"),
        ),
        out_specs=(
            P("grp", "seq", "head"),
            P("grp", "seq", "head"),
            P("grp", "head", "seq"),
            P("grp", "seq"),
        ),
        check_vma=False,
    )
```

profile of v0, /device:TPU:8, one launch (start us, length us, event | category | flops | bytes accessed | tf_op | source)
XLA Modules:
  0.0 211.8 jit_solution(9465967890961578611)
XLA Ops:
  0.6 0.9 broadcast_in_dim_reshape.3
  1.6 0.8 reshape.266
  2.4 0.7 compare_select_fusion
  3.3 1.8 reduce_window_sum.24
  5.1 1.3 broadcast_compare_fusion.3
  8.2 1.1 copy-done.1
  9.4 2.1 copy.80
  11.4 8.6 %all-to-all-start.1 = ((bf16[8,256,384]{2,0,1:T(8,128)(2,1)}), bf16[8,256,384]{2,0,1:T(8,128)(2,1)}, u32[]{:S(2)}, u32[]{:S(2)}) async-start(bf16[8,256,384]{2,0,1:T(8,128)(2,1)} %copy.80), calls=%async_computation.1 | async-start | bytes 3145728 | tf_op jit(solution)/shard_map/all_to_all | solution.py:111
  20.9 6.8 %reduce-window.6 = f32[8,6,4,128]{3,0,1,2:T(8,128)S(1)} reduce-window(f32[8,6,4,128]{3,0,1,2:T(8,128)S(1)} %copy.82, f32[]{:T(128)} %constant.91.clone.1), window={size=1x1x1x128 pad=0_0x0_0x0_0x127_0}, to_apply=%region_3.4 | reduce-window | flops 3121152 | bytes 196612 | tf_op jit(solution)/shard_map/reduce-window
  27.8 1.8 select_reduce_fusion
  29.6 5.9 %reshape_reshape.7 = bf16[8,256,6,64]{3,2,1,0:T(8,128)(2,1)} reshape(bf16[8,8,32,384]{3,2,1,0:T(8,128)(2,1)} %copy-done.1) | data formatting | bytes 3145728 | tf_op jit(solution)/shard_map/reshape;reshape | solution.py:124
  35.5 32.9 %all-gather = f32[128,6]{1,0:T(8,128)S(1)} all-gather(f32[8,6]{1,0:T(8,128)S(1)} %copy.81), channel_id=2, replica_groups=mesh['grp'=4,'seq'=16,'head'=4] {'seq'}, dimensions={0}, use_global_device_ids=true | all-gather | bytes 3264 | tf_op jit(solution)/shard_map/all_gather | solution.py:13
  68.7 1.5 while.29
  70.7 0.8 fusion.25
  71.6 1.0 select_reduce_fusion.1
  73.7 0.8 subtract_multiply_fusion
  74.5 2.8 %fusion.13 = f32[8,6,8,31]{3,1,2,0:T(8,128)S(1)} fusion(f32[8,8]{1,0:T(8,128)S(1)} %get-tuple-element.223, s32[8,8,64]{2,1,0:T(8,128)} %copy-done.8, pred[8,8,64]{2,1,0:T(8,128)(4,1)} %copy-done.14, f32[8,6,8,64]{3,2,1,0:T(8,128)} %copy-done.5, f32[8,8,31]{2,1,0:T(8,128)S(1)} %subtract_multiply_fusion), kind=kOutput, calls=%fused_computation.25 | convolution fusion | flops 9535104 | bytes 174592 | tf_op jit(solution)/shard_map/rbej,rhbj->rhbe/dot_general | solution.py:97
  77.3 0.8 broadcast_select_fusion
  78.5 3.9 %convolution_convert_fusion.1 = bf16[8,8,32,384]{3,2,1,0:T(8,128)(2,1)} fusion(bf16[8,8,64,384]{3,2,1,0:T(8,128)(2,1)} %bitcast.75, bf16[8,8,1,64]{3,2,1,0:T(2,128)(2,1)S(1)} %copy-done.7, bf16[8,8,31,64]{3,2,1,0:T(8,128)(2,1)} %copy-done.2), kind=kOutput, calls=%fused_computation.23 | convolution fusion | flops 101974016 | bytes 4980736 | tf_op jit(solution)/shard_map/rbej,rbjc->rbec/dot_general | solution.py:87
  82.3 5.9 %reshape_reshape.6 = bf16[8,256,6,64]{3,2,1,0:T(8,128)(2,1)} reshape(bf16[8,8,32,384]{3,2,1,0:T(8,128)(2,1)} %convolution_convert_fusion.1) | data formatting | bytes 3145728 | tf_op jit(solution)/shard_map/reshape;reshape | solution.py:123
  88.3 12.2 %all_gather.32 = bf16[3,32,384]{2,1,0:T(8,128)(2,1)S(1)} all-gather(bf16[3,8,384]{2,1,0:T(8,128)(2,1)S(1)} %copy-done.18), channel_id=1, replica_groups=mesh['grp'=4,'seq'=16,'head'=4] {'grp'}, dimensions={1}, use_global_device_ids=true | all-gather | bytes 92160 | tf_op jit(solution)/shard_map/all_gather | solution.py:114
  102.6 3.1 %fusion.6 = f32[8,6,1,256]{3,2,1,0:T(1,128)S(1)} fusion(bf16[8,6,64,1]{2,3,1,0:T(2,128)(2,1)S(1)} %reshape.314, bf16[8,256,6,64]{3,2,1,0:T(8,128)(2,1)} %reshape_reshape.6), kind=kOutput, calls=%fused_computation.16 | convolution fusion | flops 1572864 | bytes 1628160 | tf_op jit(solution)/shard_map/rhd,rnhd->rhn/dot_general | solution.py:126
  105.9 0.7 convert_reduce_fusion
  106.6 2.7 %fusion.4 = f32[8,6,1,64]{3,2,1,0:T(1,128)S(1)} fusion(bf16[8,256,6,64]{3,2,1,0:T(8,128)(2,1)} %reshape_reshape.7, bf16[8,6,256,1]{2,0,1,3:T(8,128)(2,1)S(1)} %bitcast.80), kind=kOutput, calls=%fused_computation.14 | convolution fusion | flops 1572864 | bytes 1609728 | tf_op jit(solution)/shard_map/rhn,rnhd->rhd/dot_general | solution.py:132
  109.3 15.6 %all-gather.3 = f32[128,6,64]{2,0,1:T(8,128)S(1)} all-gather(f32[8,6,64]{2,0,1:T(8,128)S(1)} %bitcast.78), channel_id=5, replica_groups=mesh['grp'=4,'seq'=16,'head'=4] {'seq'}, dimensions={0}, use_global_device_ids=true | all-gather | bytes 208896 | tf_op jit(solution)/shard_map/all_gather | solution.py:26
  124.9 0.7 copy-done.3
  125.7 17.0 %all-gather.2 = f32[128,6]{1,0:T(8,128)S(1)} all-gather(f32[8,6]{1,0:T(8,128)S(1)} %copy.95), channel_id=4, replica_groups=mesh['grp'=4,'seq'=16,'head'=4] {'seq'}, dimensions={0}, use_global_device_ids=true | all-gather | bytes 3264 | tf_op jit(solution)/shard_map/all_gather | solution.py:26
  142.7 14.8 %all-gather.1 = f32[128,6]{1,0:T(8,128)S(1)} all-gather(f32[8,6]{1,0:T(8,128)S(1)} %copy.94), channel_id=3, replica_groups=mesh['grp'=4,'seq'=16,'head'=4] {'seq'}, dimensions={0}, use_global_device_ids=true | all-gather | bytes 3264 | tf_op jit(solution)/shard_map/all_gather | solution.py:26
  157.5 3.5 %copy.79 = bf16[8,256,384]{2,0,1:T(8,128)(2,1)} copy(bf16[8,256,384]{2,1,0:T(8,128)(2,1)} %bitcast.73) | data formatting | bytes 3145728 | tf_op jit(solution)/shard_map/reshape | solution.py:89
  162.3 5.2 %all-to-all-start = ((bf16[8,256,384]{2,0,1:T(8,128)(2,1)}), bf16[8,256,384]{2,0,1:T(8,128)(2,1)}, u32[]{:S(2)}, u32[]{:S(2)}) async-start(bf16[8,256,384]{2,0,1:T(8,128)(2,1)} %copy.79), calls=%async_computation | async-start | bytes 3145728 | tf_op jit(solution)/shard_map/all_to_all | solution.py:110
  167.6 12.3 %while.28 = (s32[]{:T(128)}, f32[8,6]{1,0:T(8,128)S(1)}, f32[8,6]{1,0:T(8,128)S(1)}, f32[8,6,64]{2,1,0:T(8,128)S(1)}, f32[15,8,6]{2,1,0:T(8,128)}, /*index=5*/f3...) while((s32[]{:T(128)}, f32[8,6]{1,0:T(8,128)S(1)}, f32[8,6]{1,0:T(8,128)S(1)}, ...), condition=%wide.region_13.14_spmd, body=%wide.region_12.13_spmd.sunk | while | flops 9506 | bytes 63453 | solution.py:29
  167.6 0.7 fusion.46
  168.4 0.7 fusion.46
  169.2 0.7 fusion.46
  170.0 0.7 fusion.46
  170.8 0.7 fusion.46
  173.3 0.7 fusion.46
  174.1 0.7 fusion.46
  177.4 0.7 fusion.46
  179.0 0.7 fusion.46
  179.9 0.8 reshape_squeeze.2
  180.7 0.9 fusion.29
  181.6 10.8 %all_gather.39 = bf16[32,6]{1,0:T(8,128)(2,1)S(1)} all-gather(bf16[8,6]{1,0:T(8,128)(2,1)} %param.22), channel_id=1, replica_groups=mesh['grp'=4,'seq'=16,'head'=4] {'grp'}, dimensions={0}, use_global_device_ids=true | all-gather | bytes 480 | tf_op jit(solution)/shard_map/all_gather | solution.py:115
  193.3 0.7 multiply_add_fusion
  194.2 1.0 fusion.38
  195.3 11.1 %psum.7 = bf16[8,96]{1,0:T(8,128)(2,1)} all-reduce(f32[8,96]{1,0:T(8,128)S(1)} %fusion.38), channel_id=1, replica_groups=mesh['grp'=4,'seq'=16,'head'=4] {'head'}, use_global_device_ids=true, to_apply=%region_15.16 | all-reduce | flops 768 | bytes 4608 | tf_op jit(solution)/shard_map/psum | solution.py:144
  206.3 2.8 %copy.103 = bf16[8,256,384]{2,1,0:T(8,128)(2,1)} copy(bf16[8,256,384]{2,0,1:T(8,128)(2,1)} %all-to-all-done.1) | data formatting | bytes 3145728
  209.1 2.8 %copy.102 = bf16[8,256,384]{2,1,0:T(8,128)(2,1)} copy(bf16[8,256,384]{2,0,1:T(8,128)(2,1)} %all-to-all-done) | data formatting | bytes 3145728
  (186 shorter events, 16.8 us)
Async XLA Ops:
  0.6 6.3 %copy-start = (bf16[8,512,384]{2,1,0:T(8,128)(2,1)S(1)}, bf16[8,512,384]{2,1,0:T(8,128)(2,1)}, u32[]{:S(2)}) copy-start(bf16[8,512,384]{2,1,0:T(8,128)(2,1)} %param.15) | copy-start | bytes 9437188
  2.4 5.8 %copy-start.9 = (f32[8,8,64]{2,1,0:T(8,128)}, f32[8,8,64]{2,1,0:T(8,128)S(1)}, u32[]{:S(2)}) copy-start(f32[8,8,64]{2,1,0:T(8,128)S(1)} %reshape.266) | copy-start | bytes 49156
  3.2 5.0 %copy-start.14 = (pred[8,8,64]{2,1,0:T(8,128)(4,1)}, pred[8,8,64]{2,1,0:T(8,128)(4,1)S(1)}, u32[]{:S(2)}) copy-start(pred[8,8,64]{2,1,0:T(8,128)(4,1)S(1)} %broadcast_compare_fusion.1) | copy-start | bytes 12292
  3.2 4.9 %copy-start.16 = (f32[8,8]{1,0:T(8,128)}, f32[8,8]{1,0:T(8,128)S(1)}, u32[]{:S(2)}) copy-start(f32[8,8]{1,0:T(8,128)S(1)} %get-tuple-element.217) | copy-start | bytes 772
  5.0 6.4 %copy-start.8 = (s32[8,8,64]{2,1,0:T(8,128)}, s32[8,8,64]{2,1,0:T(8,128)S(1)}, u32[]{:S(2)}) copy-start(s32[8,8,64]{2,1,0:T(8,128)S(1)} %broadcast_add_fusion) | copy-start | bytes 49156
  6.7 0.8 copy-start.2
  6.9 1.3 copy-start.6
  8.2 1.1 copy-start.1
  9.4 10.7 %copy-start.22 = (s32[8]{0:T(128)S(1)}, s32[8]{0:T(128)}, u32[]{:S(2)}) copy-start(s32[8]{0:T(128)} %param.19) | copy-start | bytes 100
  9.4 10.8 %copy-start.13 = (f32[8,6,512]{2,0,1:T(8,128)S(1)}, f32[8,6,512]{2,0,1:T(8,128)}, u32[]{:S(2)}) copy-start(f32[8,6,512]{2,0,1:T(8,128)} %param.16) | copy-start | bytes 294916
  11.4 150.9 %all-to-all-start.1 = ((bf16[8,256,384]{2,0,1:T(8,128)(2,1)}), bf16[8,256,384]{2,0,1:T(8,128)(2,1)}, u32[]{:S(2)}, u32[]{:S(2)}) async-start(bf16[8,256,384]{2,0,1:T(8,128)(2,1)} %copy.80), calls=%async_computation.1 | async-start | bytes 3145728 | tf_op jit(solution)/shard_map/all_to_all | solution.py:111
  27.6 7.8 %copy-start.19 = (f32[8,6]{0,1:T(8,128)S(1)}, f32[8,6]{0,1:T(8,128)}, u32[]{:S(2)}) copy-start(f32[8,6]{0,1:T(8,128)} %get-tuple-element.220) | copy-start | bytes 580
  35.5 32.9 %copy-start.17 = (f32[8,6]{1,0:T(8,128)}, f32[8,6]{1,0:T(8,128)S(1)}, u32[]{:S(2)}) copy-start(f32[8,6]{1,0:T(8,128)S(1)} %copy.81) | copy-start | bytes 580
  70.3 8.1 %copy-start.7 = (bf16[8,8,1,64]{3,2,1,0:T(2,128)(2,1)S(1)}, bf16[8,8,1,64]{3,2,1,0:T(2,128)(2,1)}, u32[]{:S(2)}) copy-start(bf16[8,8,1,64]{3,2,1,0:T(2,128)(2,1)} %copy-done.6) | copy-start | bytes 24580
  72.6 0.7 copy-start.5
  82.3 5.9 %copy-start.18 = (bf16[3,8,384]{2,1,0:T(8,128)(2,1)S(1)}, bf16[3,8,384]{2,1,0:T(8,128)(2,1)}, u32[]{:S(2)}) copy-start(bf16[3,8,384]{2,1,0:T(8,128)(2,1)} %param.21) | copy-start | bytes 55300
  82.3 18.2 %copy-start.23 = (s32[8]{0:T(128)S(1)}, s32[8]{0:T(128)}, u32[]{:S(2)}) copy-start(s32[8]{0:T(128)} %param.20) | copy-start | bytes 100
  100.6 8.7 %copy-start.20 = (s32[1024]{0:T(1024)}, s32[1024]{0:T(1024)S(1)}, u32[]{:S(2)}) copy-start(s32[1024]{0:T(1024)S(1)} %pad_clamp_fusion) | copy-start | bytes 12292
  101.2 8.1 %copy-start.21 = (pred[8]{0:T(512)(128)(4,1)}, pred[8]{0:T(512)(128)(4,1)S(1)}, u32[]{:S(2)}) copy-start(pred[8]{0:T(512)(128)(4,1)S(1)} %compare_and_fusion) | copy-start | bytes 28
  101.3 0.6 copy-start.12
  101.9 0.6 copy-start.15
  124.9 0.7 copy-start.3
  125.7 36.5 %copy-start.4 = (f32[128,6,64]{2,0,1:T(8,128)S(1)}, f32[128,6,64]{2,0,1:T(8,128)}, u32[]{:S(2)}) copy-start(f32[128,6,64]{2,0,1:T(8,128)} %copy-done.3) | copy-start | bytes 589828
  142.7 18.9 %copy-start.10 = (f32[128,6]{1,0:T(8,128)}, f32[128,6]{1,0:T(8,128)S(1)}, u32[]{:S(2)}) copy-start(f32[128,6]{1,0:T(8,128)S(1)} %all-gather.2) | copy-start | bytes 9220
  157.5 4.7 %copy-start.11 = (f32[128,6]{1,0:T(8,128)}, f32[128,6]{1,0:T(8,128)S(1)}, u32[]{:S(2)}) copy-start(f32[128,6]{1,0:T(8,128)S(1)} %all-gather.1) | copy-start | bytes 9220
  162.2 5.3 %slice-start = ((f32[128,6]{1,0:T(8,128)}), f32[8,6]{1,0:T(8,128)S(1)}, s32[]{:S(2)}) async-start(f32[128,6]{1,0:T(8,128)} %copy-done.10), calls=%async_computation.2 | async-start | bytes 8192 | tf_op jit(solution)/shard_map/slice | solution.py:27
  162.3 5.3 %slice-start.1 = ((f32[128,6]{1,0:T(8,128)}), f32[8,6]{1,0:T(8,128)S(1)}, s32[]{:S(2)}) async-start(f32[128,6]{1,0:T(8,128)} %copy-done.11), calls=%async_computation.3 | async-start | bytes 8192 | tf_op jit(solution)/shard_map/slice | solution.py:27
  162.3 46.8 %all-to-all-start = ((bf16[8,256,384]{2,0,1:T(8,128)(2,1)}), bf16[8,256,384]{2,0,1:T(8,128)(2,1)}, u32[]{:S(2)}, u32[]{:S(2)}) async-start(bf16[8,256,384]{2,0,1:T(8,128)(2,1)} %copy.79), calls=%async_computation | async-start | bytes 3145728 | tf_op jit(solution)/shard_map/all_to_all | solution.py:110
where the time goes:
time: 214 us; the launch traced here: 212 us
  blocking collectives  114 us (53%)
  local copies, waits for them, and re-layouts  35.5 us (17%)
  other arithmetic  32.4 us (15%)
  matrix products  14.2 us (7%)
  starting transfers between devices  13.8 us (6%)
    all_gather x3, blocking collectives, merged(): pieces = jax.tree.map(lambda part: lax.all_gather(part, axis), value)  47.3 us
    all_gather x1, blocking collectives, carried_in(): pieces = lax.all_gather(value, axis)  32.9 us
    all_gather x1, blocking collectives, shards(): lax.all_gather(fresh, 'grp', axis=1, tiled=True)  12.2 us
    psum x1, blocking collectives, shards(): layer_out = lax.psum(partial_out, 'head').astype(jnp.bfloat16)  11.1 us
    all_gather x1, blocking collectives, shards(): lax.all_gather(new_forget, 'grp', axis=0, tiled=True)  10.8 us
    add x15, other arithmetic, merge_parts(): sum_one * scale_one + sum_two * scale_two  10.6 us
    unnamed x50, local copies, waits for them, and re-layouts  9.61 us
    all_to_all x1, starting transfers between devices, shards(): lax.all_to_all(packed_values, 'seq', split_axis=1, concat_axis=1, tiled=T...  8.61 us
  transfers between devices with their start and end apart: 2, of which 0 were waited for; matrix products, arithmetic and copies ran while one was open for 31% of the time, Pallas kernels for 0%

commit v1 on v0

--- a/solution.py
+++ b/solution.py
@@ -106,9 +106,16 @@
         req_dev, heads_dev, rows_dev
     )
     compact_decay = jnp.exp(slot_log)
+
+    def work_trees(local_values):
+        moved = jnp.split(local_values, lax.axis_size("seq"), axis=1)
+        res = jnp.stack(moved)
+        x_next = jnp.concatenate(lax.all_to_all(res, "seq", 0, 0), axis=1)
+        return x_next
+
     dealt_keys, dealt_values = (
         lax.all_to_all(packed_keys, "seq", split_axis=1, concat_axis=1, tiled=True),
-        lax.all_to_all(packed_values, "seq", split_axis=1, concat_axis=1, tiled=True),
+        work_trees(packed_values),
     )
     arrived, arrived_forget = (
         lax.all_gather(fresh, "grp", axis=1, tiled=True),

time: 214 us -> 219 us (1.023)
  local copies, waits for them, and re-layouts: 35.5 us -> 42.3 us
    unnamed x50 -> x70, local copies, waits for them, and re-layouts: 9.61 us -> 15.1 us
  transfers between devices with their start and end apart: 2 -> 2, of which waited for: 0 -> 0; matrix products, arithmetic and copies ran while one was open for 31% -> 30% of each run, Pallas kernels for 0% -> 0%
where the time goes in v1:
time: 219 us; the launch traced here: 218 us
  blocking collectives  114 us (52%)
  local copies, waits for them, and re-layouts  42.3 us (19%)
  other arithmetic  31.7 us (14%)
  matrix products  14.2 us (6%)
  starting transfers between devices  14 us (6%)
    all_gather x3, blocking collectives, merged(): pieces = jax.tree.map(lambda part: lax.all_gather(part, axis), value)  47 us
    all_gather x1, blocking collectives, carried_in(): pieces = lax.all_gather(value, axis)  32.9 us
    unnamed x70, local copies, waits for them, and re-layouts  15.1 us
    all_gather x1, blocking collectives, shards(): lax.all_gather(fresh, 'grp', axis=1, tiled=True)  12.2 us
    psum x1, blocking collectives, shards(): layer_out = lax.psum(partial_out, 'head').astype(jnp.bfloat16)  11.1 us
    all_gather x1, blocking collectives, shards(): lax.all_gather(new_forget, 'grp', axis=0, tiled=True)  10.8 us
    add x15, other arithmetic, merge_parts(): sum_one * scale_one + sum_two * scale_two  10.6 us
    all_to_all x1, starting transfers between devices, work_trees(): x_next = jnp.concatenate(lax.all_to_all(res, 'seq', 0, 0), axis=1)  8.75 us
  transfers between devices with their start and end apart: 2, of which 0 were waited for; matrix products, arithmetic and copies ran while one was open for 30% of the time, Pallas kernels for 0%

profile of v1, /device:TPU:8, one launch (start us, length us, event | category | flops | bytes accessed | tf_op | source)
XLA Modules:
  0.0 217.8 jit_solution(7801411780749923550)
XLA Ops:
  0.6 0.9 broadcast_in_dim_reshape.3
  1.6 0.8 reshape.272
  2.4 0.7 compare_select_fusion
  3.3 1.8 reduce_window_sum.24
  5.1 1.3 broadcast_compare_fusion.3
  7.7 0.7 fusion.38
  18.2 8.7 %all-to-all-start.1 = ((bf16[16,8,16,384]{3,2,1,0:T(8,128)(2,1)}), bf16[16,8,16,384]{3,2,1,0:T(8,128)(2,1)}, u32[]{:S(2)}, u32[]{:S(2)}) async-start(bf16[16,8,16,384]{3,2,1,0:T(8,128)(2,1)} %fusion.23), calls=%async_computation.1 | async-start | bytes 3145728 | tf_op jit(solution)/shard_map/all_to_all | solution.py:113
  27.8 6.8 %reduce-window.6 = f32[8,6,4,128]{3,0,1,2:T(8,128)S(1)} reduce-window(f32[8,6,4,128]{3,0,1,2:T(8,128)S(1)} %copy.83, f32[]{:T(128)} %constant.91.clone.1), window={size=1x1x1x128 pad=0_0x0_0x0_0x127_0}, to_apply=%region_3.4 | reduce-window | flops 3121152 | bytes 196612 | tf_op jit(solution)/shard_map/reduce-window
  34.6 1.8 select_reduce_fusion
  36.5 5.9 %reshape_reshape.7 = bf16[8,256,6,64]{3,2,1,0:T(8,128)(2,1)} reshape(bf16[8,8,32,384]{3,2,1,0:T(8,128)(2,1)} %copy-done.1) | data formatting | bytes 3145728 | tf_op jit(solution)/shard_map/reshape;reshape | solution.py:131
  42.4 32.9 %all-gather = f32[128,6]{1,0:T(8,128)S(1)} all-gather(f32[8,6]{1,0:T(8,128)S(1)} %copy.82), channel_id=2, replica_groups=mesh['grp'=4,'seq'=16,'head'=4] {'seq'}, dimensions={0}, use_global_device_ids=true | all-gather | bytes 3264 | tf_op jit(solution)/shard_map/all_gather | solution.py:13
  75.6 1.5 while.29
  77.6 0.8 fusion.41
  78.5 1.0 select_reduce_fusion.1
  80.6 0.8 subtract_multiply_fusion
  81.4 2.8 %fusion.13 = f32[8,6,8,31]{3,1,2,0:T(8,128)S(1)} fusion(f32[8,8]{1,0:T(8,128)S(1)} %get-tuple-element.223, s32[8,8,64]{2,1,0:T(8,128)S(1)} %copy-done.9, pred[8,8,64]{2,1,0:T(8,128)(4,1)S(1)} %copy-done.16, f32[8,6,8,64]{3,2,1,0:T(8,128)} %copy-done.5, f32[8,8,31]{2,1,0:T(8,128)S(1)} %subtract_multiply_fusion), kind=kOutput, calls=%fused_computation.25 | convolution fusion | flops 9535104 | bytes 174592 | tf_op jit(solution)/shard_map/rbej,rhbj->rhbe/dot_general | solution.py:97
  84.7 3.9 %convolution_convert_fusion.1 = bf16[8,8,32,384]{3,2,1,0:T(8,128)(2,1)} fusion(bf16[8,8,64,384]{3,2,1,0:T(8,128)(2,1)} %bitcast.156, bf16[8,8,1,64]{3,2,1,0:T(2,128)(2,1)S(1)} %copy-done.7, bf16[8,8,31,64]{3,2,1,0:T(8,128)(2,1)} %copy-done.2), kind=kOutput, calls=%fused_computation.23 | convolution fusion | flops 101974016 | bytes 4980736 | tf_op jit(solution)/shard_map/rbej,rbjc->rbec/dot_general | solution.py:87
  88.6 5.9 %reshape_reshape.6 = bf16[8,256,6,64]{3,2,1,0:T(8,128)(2,1)} reshape(bf16[8,8,32,384]{3,2,1,0:T(8,128)(2,1)} %convolution_convert_fusion.1) | data formatting | bytes 3145728 | tf_op jit(solution)/shard_map/reshape;reshape | solution.py:130
  94.5 12.2 %all_gather.32 = bf16[3,32,384]{2,1,0:T(8,128)(2,1)S(1)} all-gather(bf16[3,8,384]{2,1,0:T(8,128)(2,1)S(1)} %copy-done.20), channel_id=1, replica_groups=mesh['grp'=4,'seq'=16,'head'=4] {'grp'}, dimensions={1}, use_global_device_ids=true | all-gather | bytes 92160 | tf_op jit(solution)/shard_map/all_gather | solution.py:121
  108.9 3.1 %fusion.6 = f32[8,6,1,256]{3,2,1,0:T(1,128)S(1)} fusion(bf16[8,6,64,1]{2,3,1,0:T(2,128)(2,1)S(1)} %reshape.322, bf16[8,256,6,64]{3,2,1,0:T(8,128)(2,1)} %reshape_reshape.6), kind=kOutput, calls=%fused_computation.16 | convolution fusion | flops 1572864 | bytes 1628160 | tf_op jit(solution)/shard_map/rhd,rnhd->rhn/dot_general | solution.py:133
  112.2 0.7 convert_reduce_fusion
  112.9 2.7 %fusion.4 = f32[8,6,1,64]{3,2,1,0:T(1,128)S(1)} fusion(bf16[8,256,6,64]{3,2,1,0:T(8,128)(2,1)} %reshape_reshape.7, bf16[8,6,256,1]{2,0,1,3:T(8,128)(2,1)S(1)} %bitcast.162), kind=kOutput, calls=%fused_computation.14 | convolution fusion | flops 1572864 | bytes 1609728 | tf_op jit(solution)/shard_map/rhn,rnhd->rhd/dot_general | solution.py:139
  115.6 15.6 %all-gather.3 = f32[128,6,64]{2,0,1:T(8,128)S(1)} all-gather(f32[8,6,64]{2,0,1:T(8,128)S(1)} %bitcast.160), channel_id=5, replica_groups=mesh['grp'=4,'seq'=16,'head'=4] {'seq'}, dimensions={0}, use_global_device_ids=true | all-gather | bytes 208896 | tf_op jit(solution)/shard_map/all_gather | solution.py:26
  131.2 0.7 copy-done.3
  132.0 16.8 %all-gather.2 = f32[128,6]{1,0:T(8,128)S(1)} all-gather(f32[8,6]{1,0:T(8,128)S(1)} %copy.96), channel_id=4, replica_groups=mesh['grp'=4,'seq'=16,'head'=4] {'seq'}, dimensions={0}, use_global_device_ids=true | all-gather | bytes 3264 | tf_op jit(solution)/shard_map/all_gather | solution.py:26
  148.8 14.6 %all-gather.1 = f32[128,6]{1,0:T(8,128)S(1)} all-gather(f32[8,6]{1,0:T(8,128)S(1)} %copy.95), channel_id=3, replica_groups=mesh['grp'=4,'seq'=16,'head'=4] {'seq'}, dimensions={0}, use_global_device_ids=true | all-gather | bytes 3264 | tf_op jit(solution)/shard_map/all_gather | solution.py:26
  163.4 3.5 %copy.80 = bf16[8,256,384]{2,0,1:T(8,128)(2,1)} copy(bf16[8,256,384]{2,1,0:T(8,128)(2,1)} %bitcast.139) | data formatting | bytes 3145728 | tf_op jit(solution)/shard_map/reshape | solution.py:89
  168.3 5.2 %all-to-all-start = ((bf16[8,256,384]{2,0,1:T(8,128)(2,1)}), bf16[8,256,384]{2,0,1:T(8,128)(2,1)}, u32[]{:S(2)}, u32[]{:S(2)}) async-start(bf16[8,256,384]{2,0,1:T(8,128)(2,1)} %copy.80), calls=%async_computation | async-start | bytes 3145728 | tf_op jit(solution)/shard_map/all_to_all | solution.py:117
  173.5 12.3 %while.28 = (s32[]{:T(128)}, f32[8,6]{1,0:T(8,128)S(1)}, f32[8,6]{1,0:T(8,128)S(1)}, f32[8,6,64]{2,1,0:T(8,128)S(1)}, f32[15,8,6]{2,1,0:T(8,128)}, /*index=5*/f3...) while((s32[]{:T(128)}, f32[8,6]{1,0:T(8,128)S(1)}, f32[8,6]{1,0:T(8,128)S(1)}, ...), condition=%wide.region_13.14_spmd, body=%wide.region_12.13_spmd.sunk | while | flops 9506 | bytes 63453 | solution.py:29
  173.6 0.7 fusion.62
  174.4 0.7 fusion.62
  175.2 0.7 fusion.62
  176.0 0.7 fusion.62
  176.9 0.7 fusion.62
  177.7 0.7 fusion.62
  178.5 0.7 fusion.62
  179.3 0.7 fusion.62
  180.1 0.7 fusion.62
  180.9 0.7 fusion.62
  184.2 0.7 fusion.62
  185.8 0.8 reshape_squeeze.2
  186.6 0.9 fusion.45
  187.6 10.8 %all_gather.39 = bf16[32,6]{1,0:T(8,128)(2,1)S(1)} all-gather(bf16[8,6]{1,0:T(8,128)(2,1)} %param.22), channel_id=1, replica_groups=mesh['grp'=4,'seq'=16,'head'=4] {'grp'}, dimensions={0}, use_global_device_ids=true | all-gather | bytes 480 | tf_op jit(solution)/shard_map/all_gather | solution.py:122
  199.3 0.7 multiply_add_fusion
  200.2 1.0 fusion.54
  201.2 11.1 %psum.7 = bf16[8,96]{1,0:T(8,128)(2,1)} all-reduce(f32[8,96]{1,0:T(8,128)S(1)} %fusion.54), channel_id=1, replica_groups=mesh['grp'=4,'seq'=16,'head'=4] {'head'}, use_global_device_ids=true, to_apply=%region_15.16 | all-reduce | flops 768 | bytes 4608 | tf_op jit(solution)/shard_map/psum | solution.py:151
  212.3 2.7 %copy.81 = bf16[8,16,16,384]{3,2,1,0:T(8,128)(2,1)} copy(bf16[8,16,16,384]{3,2,0,1:T(8,128)(2,1)} %bitcast.23) | data formatting | bytes 3145728 | tf_op jit(solution)/shard_map/reshape | solution.py:113
  215.0 2.8 %copy.103 = bf16[8,256,384]{2,1,0:T(8,128)(2,1)} copy(bf16[8,256,384]{2,0,1:T(8,128)(2,1)} %all-to-all-done) | data formatting | bytes 3145728
  (207 shorter events, 24.8 us)
Async XLA Ops:
  0.6 6.3 %copy-start = (bf16[8,512,384]{2,1,0:T(8,128)(2,1)S(1)}, bf16[8,512,384]{2,1,0:T(8,128)(2,1)}, u32[]{:S(2)}) copy-start(bf16[8,512,384]{2,1,0:T(8,128)(2,1)} %param.15) | copy-start | bytes 9437188
  2.4 5.2 %copy-start.10 = (f32[8,8,64]{2,1,0:T(8,128)}, f32[8,8,64]{2,1,0:T(8,128)S(1)}, u32[]{:S(2)}) copy-start(f32[8,8,64]{2,1,0:T(8,128)S(1)} %reshape.272) | copy-start | bytes 49156
  3.2 4.5 %copy-start.15 = (pred[8,8,64]{2,1,0:T(8,128)(4,1)}, pred[8,8,64]{2,1,0:T(8,128)(4,1)S(1)}, u32[]{:S(2)}) copy-start(pred[8,8,64]{2,1,0:T(8,128)(4,1)S(1)} %broadcast_compare_fusion.1) | copy-start | bytes 12292
  3.2 4.4 %copy-start.18 = (f32[8,8]{1,0:T(8,128)}, f32[8,8]{1,0:T(8,128)S(1)}, u32[]{:S(2)}) copy-start(f32[8,8]{1,0:T(8,128)S(1)} %get-tuple-element.217) | copy-start | bytes 772
  5.0 2.6 %copy-start.8 = (s32[8,8,64]{2,1,0:T(8,128)}, s32[8,8,64]{2,1,0:T(8,128)S(1)}, u32[]{:S(2)}) copy-start(s32[8,8,64]{2,1,0:T(8,128)S(1)} %broadcast_add_fusion) | copy-start | bytes 49156
  6.7 1.0 copy-start.2
  6.9 0.8 copy-start.6
  7.7 9.9 %copy-start.1 = (bf16[8,8,32,384]{3,2,1,0:T(8,128)(2,1)}, bf16[8,8,32,384]{3,2,1,0:T(8,128)(2,1)S(1)}, u32[]{:S(2)}) copy-start(bf16[8,8,32,384]{3,2,1,0:T(8,128)(2,1)S(1)} %convolution_convert_fusion) | copy-start | bytes 4718596
  18.2 8.8 %copy-start.25 = (s32[8]{0:T(128)S(1)}, s32[8]{0:T(128)}, u32[]{:S(2)}) copy-start(s32[8]{0:T(128)} %param.19) | copy-start | bytes 100
  18.2 8.9 %copy-start.14 = (f32[8,6,512]{2,0,1:T(8,128)S(1)}, f32[8,6,512]{2,0,1:T(8,128)}, u32[]{:S(2)}) copy-start(f32[8,6,512]{2,0,1:T(8,128)} %param.16) | copy-start | bytes 294916
  18.2 150.1 %all-to-all-start.1 = ((bf16[16,8,16,384]{3,2,1,0:T(8,128)(2,1)}), bf16[16,8,16,384]{3,2,1,0:T(8,128)(2,1)}, u32[]{:S(2)}, u32[]{:S(2)}) async-start(bf16[16,8,16,384]{3,2,1,0:T(8,128)(2,1)} %fusion.23), calls=%async_computation.1 | async-start | bytes 3145728 | tf_op jit(solution)/shard_map/all_to_all | solution.py:113
  36.5 5.9 %copy-start.21 = (f32[8,6]{0,1:T(8,128)S(1)}, f32[8,6]{0,1:T(8,128)}, u32[]{:S(2)}) copy-start(f32[8,6]{0,1:T(8,128)} %get-tuple-element.220) | copy-start | bytes 580
  42.4 32.9 %copy-start.19 = (f32[8,6]{1,0:T(8,128)}, f32[8,6]{1,0:T(8,128)S(1)}, u32[]{:S(2)}) copy-start(f32[8,6]{1,0:T(8,128)S(1)} %copy.82) | copy-start | bytes 580
  77.2 4.2 %copy-start.9 = (s32[8,8,64]{2,1,0:T(8,128)S(1)}, s32[8,8,64]{2,1,0:T(8,128)}, u32[]{:S(2)}) copy-start(s32[8,8,64]{2,1,0:T(8,128)} %copy-done.8) | copy-start | bytes 49156
  77.2 4.2 %copy-start.16 = (pred[8,8,64]{2,1,0:T(8,128)(4,1)S(1)}, pred[8,8,64]{2,1,0:T(8,128)(4,1)}, u32[]{:S(2)}) copy-start(pred[8,8,64]{2,1,0:T(8,128)(4,1)} %copy-done.15) | copy-start | bytes 12292
  77.2 7.0 %copy-start.23 = (pred[8,8]{1,0:T(8,128)(4,1)S(1)}, pred[8,8]{1,0:T(8,128)(4,1)}, u32[]{:S(2)}) copy-start(pred[8,8]{1,0:T(8,128)(4,1)} %get-tuple-element.222) | copy-start | bytes 196
  79.5 0.7 copy-start.5
  81.4 3.3 %copy-start.7 = (bf16[8,8,1,64]{3,2,1,0:T(2,128)(2,1)S(1)}, bf16[8,8,1,64]{3,2,1,0:T(2,128)(2,1)}, u32[]{:S(2)}) copy-start(bf16[8,8,1,64]{3,2,1,0:T(2,128)(2,1)} %copy-done.6) | copy-start | bytes 24580
  88.6 5.9 %copy-start.20 = (bf16[3,8,384]{2,1,0:T(8,128)(2,1)S(1)}, bf16[3,8,384]{2,1,0:T(8,128)(2,1)}, u32[]{:S(2)}) copy-start(bf16[3,8,384]{2,1,0:T(8,128)(2,1)} %param.21) | copy-start | bytes 55300
  88.6 18.2 %copy-start.26 = (s32[8]{0:T(128)S(1)}, s32[8]{0:T(128)}, u32[]{:S(2)}) copy-start(s32[8]{0:T(128)} %param.20) | copy-start | bytes 100
  106.8 5.1 %copy-start.22 = (s32[1024]{0:T(1024)}, s32[1024]{0:T(1024)S(1)}, u32[]{:S(2)}) copy-start(s32[1024]{0:T(1024)S(1)} %pad_clamp_fusion) | copy-start | bytes 12292
  107.4 4.5 %copy-start.24 = (pred[8]{0:T(512)(128)(4,1)}, pred[8]{0:T(512)(128)(4,1)S(1)}, u32[]{:S(2)}) copy-start(pred[8]{0:T(512)(128)(4,1)S(1)} %compare_and_fusion) | copy-start | bytes 28
  107.5 0.6 copy-start.13
  108.2 0.6 copy-start.17
  131.2 0.7 copy-start.3
  148.8 18.1 %copy-start.11 = (f32[128,6]{1,0:T(8,128)}, f32[128,6]{1,0:T(8,128)S(1)}, u32[]{:S(2)}) copy-start(f32[128,6]{1,0:T(8,128)S(1)} %all-gather.2) | copy-start | bytes 9220
  163.4 4.2 %copy-start.12 = (f32[128,6]{1,0:T(8,128)}, f32[128,6]{1,0:T(8,128)S(1)}, u32[]{:S(2)}) copy-start(f32[128,6]{1,0:T(8,128)S(1)} %all-gather.1) | copy-start | bytes 9220
  163.4 4.8 %copy-start.4 = (f32[128,6,64]{2,0,1:T(8,128)S(1)}, f32[128,6,64]{2,0,1:T(8,128)}, u32[]{:S(2)}) copy-start(f32[128,6,64]{2,0,1:T(8,128)} %copy-done.3) | copy-start | bytes 589828
  168.3 5.3 %slice-start = ((f32[128,6]{1,0:T(8,128)}), f32[8,6]{1,0:T(8,128)S(1)}, s32[]{:S(2)}) async-start(f32[128,6]{1,0:T(8,128)} %copy-done.11), calls=%async_computation.2 | async-start | bytes 8192 | tf_op jit(solution)/shard_map/slice | solution.py:27
  168.3 5.3 %slice-start.1 = ((f32[128,6]{1,0:T(8,128)}), f32[8,6]{1,0:T(8,128)S(1)}, s32[]{:S(2)}) async-start(f32[128,6]{1,0:T(8,128)} %copy-done.12), calls=%async_computation.3 | async-start | bytes 8192 | tf_op jit(solution)/shard_map/slice | solution.py:27
  168.3 46.7 %all-to-all-start = ((bf16[8,256,384]{2,0,1:T(8,128)(2,1)}), bf16[8,256,384]{2,0,1:T(8,128)(2,1)}, u32[]{:S(2)}, u32[]{:S(2)}) async-start(bf16[8,256,384]{2,0,1:T(8,128)(2,1)} %copy.80), calls=%async_computation | async-start | bytes 3145728 | tf_op jit(solution)/shard_map/all_to_all | solution.py:117
